TPU v7x, 256 devices: a whole 4x4x8 slice. The times are simulated.
256 devices in a mesh: island: 32 (over x_hi, z, core), fsdp: 8 (over y, x_lo).
Axes of the slice: x: 4 (x_hi: 2, x_lo: 2; x = x_hi * 2 + x_lo), y: 4, z: 8, core: 2. Of those that a mesh axis runs over, the one named last changes fastest.
Arguments:
- activations: bfloat16 [32768, 8192], P(('island', 'fsdp')), may hold values from -6 to 6
- cotangent: bfloat16 [32768, 1024], P(('island', 'fsdp')), may hold values from -6 to 6
- inner_weight: bfloat16 [32, 8192, 1024], P('island', 'fsdp'), may hold values from -0.125 to 0.125
- outer_weight: float32 [8192, 1024], P(('fsdp', 'island')), may hold values from -0.0625 to 0.0625
- outer_momentum: float32 [8192, 1024], P(('fsdp', 'island')), may hold values from -0.06 to 0.06
- next_activations: bfloat16 [32768, 8192], P(('island', 'fsdp')), may hold values from -6 to 6
Outputs:
- input_grad: bfloat16 [32768, 8192], P(('island', 'fsdp'))
- next_keys: bfloat16 [32768, 1024], P(('island', 'fsdp'))
- new_outer: float32 [8192, 1024], P(('fsdp', 'island'))
- new_momentum: float32 [8192, 1024], P(('fsdp', 'island'))
All inputs are finite; a program needn't handle non-finite values.
Results may differ from a plain program's by a relative error of at most 0.0049.
Values may be sent and summed in bfloat16 or wider, within the bound.
A program may use at most 128 MiB of HBM per device.

v0:
```python
import jax
import jax.numpy as jnp
from jax import lax
from jax.sharding import PartitionSpec as P

inner_rate = 1.2
outer_rate = 0.7
nesterov = 0.9


def local(activations, cotangent, inner_weight, outer_weight, outer_momentum, next_activations):
    fsdp_count = lax.axis_size("fsdp")
    island_count = lax.axis_size("island")
    tok_rows = activations.shape[0]
    own_weight = inner_weight[0]
    island_cotangent = lax.all_gather(cotangent, "fsdp", axis=0, tiled=True)
    column_block = lax.all_to_all(activations, "fsdp", split_axis=1, concat_axis=0, tiled=True)
    next_block = lax.all_to_all(next_activations, "fsdp", split_axis=1, concat_axis=0, tiled=True)
    weight_grad = lax.dot_general(
        column_block, island_cotangent, (((0,), (0,)), ((), ())), preferred_element_type=jnp.float32
    ) / (tok_rows * fsdp_count)
    inner_new = own_weight.astype(jnp.float32) - inner_rate * weight_grad
    summed = lax.psum_scatter(inner_new, "island", scatter_dimension=0, tiled=True)
    grad_columns = lax.dot_general(
        island_cotangent, own_weight, (((1,), (1,)), ((), ())), preferred_element_type=jnp.float32
    ).astype(jnp.bfloat16)
    input_grad = lax.all_to_all(grad_columns, "fsdp", split_axis=0, concat_axis=1, tiled=True)
    pseudo_grad = outer_weight - summed / island_count
    new_momentum = nesterov * outer_momentum + pseudo_grad
    new_outer = outer_weight - outer_rate * (pseudo_grad + nesterov * new_momentum)
    new_share = new_outer.astype(jnp.bfloat16)
    island_block = lax.all_gather(new_share, "island", axis=0, tiled=True)
    partial = jnp.dot(next_block, island_block, preferred_element_type=jnp.float32).astype(jnp.bfloat16)
    pieces = lax.all_to_all(partial.reshape(fsdp_count, tok_rows, -1), "fsdp", split_axis=0, concat_axis=0, tiled=True)
    next_keys = jnp.sum(pieces.astype(jnp.float32), axis=0)
    return (input_grad, next_keys.astype(jnp.bfloat16), new_outer, new_momentum)


def solution(mesh):
    in_specs = (
        P(("island", "fsdp"), None),
        P(("island", "fsdp"), None),
        P("island", "fsdp", None),
        P(("fsdp", "island"), None),
        P(("fsdp", "island"), None),
        P(("island", "fsdp"), None),
    )
    out_specs = (
        P(("island", "fsdp"), None),
        P(("island", "fsdp"), None),
        P(("fsdp", "island"), None),
        P(("fsdp", "island"), None),
    )
    return jax.shard_map(local, mesh=mesh, in_specs=in_specs, out_specs=out_specs, check_vma=False)
```

profile of v0, /device:TPU:8, one launch (start us, length us, event | category | flops | bytes accessed | tf_op | source)
XLA Modules:
  0.0 347.6 jit_solution(16094766535880656538)
XLA Ops:
  7.2 0.7 all-gather.3.cloned.1.call-update
  7.9 0.0 reduce-scatter.2.cloned.1.call-start
  7.9 4.1 %copy.13 = bf16[128,8192]{0,1:T(8,128)(2,1)} copy(bf16[128,8192]{1,0:T(8,128)(2,1)} %param.6) | data formatting | bytes 4194304 | tf_op args[0]
  12.0 47.9 %all_to_all.62 = bf16[128,8,1024]{0,2,1:T(8,128)(2,1)S(1)} all-to-all(bf16[128,8,1024]{0,2,1:T(8,128)(2,1)} %bitcast.28), channel_id=1, replica_groups=mesh['island'=32,'fsdp'=8] {'fsdp'}, dimensions={1} | all-to-all | bytes 4194304 | tf_op jit(solution)/shard_map/all_to_all | solution.py:17
  59.9 2.6 copy.14
  62.5 19.7 %all-gather.3.cloned.1.call-done = bf16[1024,1024]{1,0:T(8,128)(2,1)} async-done(((bf16[128,1024]{1,0:T(8,128)(2,1)}), bf16[1024,1024]{1,0:T(8,128)(2,1)}) %all-gather.3.cloned.1.call-update) | async-done | bytes 2097168 | tf_op jit(solution)/shard_map/all_gather | solution.py:16
  82.1 7.2 %multiply_subtract_fusion = f32[1024,1024]{1,0:T(8,128)} fusion(bf16[1024,1024]{1,0:T(8,128)(2,1)} %bitcast.33, bf16[1024,1024]{1,0:T(8,128)(2,1)} %all-gather.3.cloned.1.call-done, bf16[1,1024,1024]{2,1,0:T(8,128)(2,1)} %param.8), kind=kOutput, calls=%fused_computation | convolution fusion | flops 2150629376 | bytes 10485760 | tf_op jit(solution)/shard_map/dot_general | solution.py:19
  89.4 0.0 all-gather.5.cloned.1.call-start
  89.4 130.3 %reduce-scatter.2.cloned.1.call-done = f32[32,1024]{1,0:T(8,128)} async-done(((f32[1024,1024]{1,0:T(8,128)}), f32[32,1024]{1,0:T(8,128)}) %reduce-scatter.2.cloned.1.call-update) | async-done | bytes 131088 | tf_op jit(solution)/shard_map/reduce_scatter | solution.py:23
  219.7 1.7 fusion.5
  221.4 2.4 copy.15
  223.8 4.7 %all-to-all-start.2 = ((bf16[128,8,1024]{0,2,1:T(8,128)(2,1)}), bf16[128,8,1024]{0,2,1:T(8,128)(2,1)S(1)}, u32[]{:S(2)}, u32[]{:S(2)}) async-start(bf16[128,8,1024]{0,2,1:T(8,128)(2,1)} %bitcast.26), calls=%async_computation.3 | async-start | bytes 4194304 | tf_op jit(solution)/shard_map/all_to_all | solution.py:18
  228.6 5.9 %fusion.2 = bf16[1024,1024]{1,0:T(8,128)(2,1)} fusion(bf16[1024,1024]{1,0:T(8,128)(2,1)} %all-gather.3.cloned.1.call-done, bf16[1,1024,1024]{2,1,0:T(8,128)(2,1)} %param.8), kind=kOutput, calls=%fused_computation.3 | convolution fusion | flops 2148532224 | bytes 6291456 | tf_op jit(solution)/shard_map/dot_general | solution.py:24
  234.5 15.6 %all-to-all-done.2 = bf16[128,8,1024]{0,2,1:T(8,128)(2,1)S(1)} async-done(((bf16[128,8,1024]{0,2,1:T(8,128)(2,1)}), bf16[128,8,1024]{0,2,1:T(8,128)(2,1)S(1)}, u32[]{:S(2)}, u32[]{:S(2)}) %all-to-all-start.2) | async-done | bytes 2097184 | tf_op jit(solution)/shard_map/all_to_all | solution.py:18
  250.1 1.3 copy-done.1
  251.4 5.3 %all-to-all-start = ((bf16[8,128,1024]{2,1,0:T(8,128)(2,1)}), bf16[8,128,1024]{2,1,0:T(8,128)(2,1)S(1)}, u32[]{:S(2)}, u32[]{:S(2)}) async-start(bf16[8,128,1024]{2,1,0:T(8,128)(2,1)} %bitcast.29), calls=%async_computation | async-start | bytes 4194304 | tf_op jit(solution)/shard_map/all_to_all | solution.py:27
  256.7 3.9 %copy.16 = bf16[8,128,1024]{2,1,0:T(8,128)(2,1)} copy(bf16[8,128,1024]{1,2,0:T(8,128)(2,1)} %bitcast.25) | data formatting | bytes 4194304 | tf_op jit(solution)/shard_map/all_to_all | solution.py:18
  260.7 41.0 %all-gather.5.cloned.1.call-done = bf16[1024,1024]{1,0:T(8,128)(2,1)} async-done(((bf16[32,1024]{1,0:T(8,128)(2,1)}), bf16[1024,1024]{1,0:T(8,128)(2,1)}) %all-gather.5.cloned.1.call-update) | async-done | bytes 2097168 | tf_op jit(solution)/shard_map/all_gather | solution.py:32
  301.6 5.9 %convolution_convert_fusion = bf16[1024,1024]{0,1:T(8,128)(2,1)} fusion(bf16[1024,1024]{1,0:T(8,128)(2,1)} %bitcast.32, bf16[1024,1024]{1,0:T(8,128)(2,1)} %all-gather.5.cloned.1.call-done), kind=kOutput, calls=%fused_computation.4 | convolution fusion | flops 2148532224 | bytes 6291456 | tf_op jit(solution)/shard_map/dot_general | solution.py:33
  307.5 1.3 copy-done
  308.8 5.5 %all-to-all-start.3 = ((bf16[8,128,1024]{2,1,0:T(8,128)(2,1)}), bf16[8,128,1024]{2,1,0:T(8,128)(2,1)S(1)}, u32[]{:S(2)}, u32[]{:S(2)}) async-start(bf16[8,128,1024]{2,1,0:T(8,128)(2,1)} %bitcast.31), calls=%async_computation.4 | async-start | bytes 4194304 | tf_op jit(solution)/shard_map/all_to_all | solution.py:34
  314.3 3.1 copy.17
  317.5 22.5 %all-to-all-done.3 = bf16[8,128,1024]{2,1,0:T(8,128)(2,1)S(1)} async-done(((bf16[8,128,1024]{2,1,0:T(8,128)(2,1)}), bf16[8,128,1024]{2,1,0:T(8,128)(2,1)S(1)}, u32[]{:S(2)}, u32[]{:S(2)}) %all-to-all-start.3) | async-done | bytes 2097184 | tf_op jit(solution)/shard_map/all_to_all | solution.py:34
  340.0 1.1 reduce_sum.12
  (12 shorter events, 0.1 us)
Async XLA Ops:
  7.2 75.0 %all-gather.3.cloned.1.call-start = ((), (), s32[]{:S(2)}) async-start(), calls=%async_computation.5 | async-start | bytes 2359296 | tf_op jit(solution)/shard_map/all_gather | solution.py:16
  7.9 211.8 %reduce-scatter.2.cloned.1.call-start = ((), (), s32[]{:S(2)}) async-start(), calls=%async_computation.6 | async-start | bytes 4325376 | tf_op jit(solution)/shard_map/reduce_scatter | solution.py:23
  89.3 130.4 %copy-start.3 = (f32[32,1024]{1,0:T(8,128)S(1)}, f32[32,1024]{1,0:T(8,128)}, u32[]{:S(2)}) copy-start(f32[32,1024]{1,0:T(8,128)} %param.9) | copy-start | bytes 393220
  89.3 130.4 %copy-start.4 = (f32[32,1024]{1,0:T(8,128)S(1)}, f32[32,1024]{1,0:T(8,128)}, u32[]{:S(2)}) copy-start(f32[32,1024]{1,0:T(8,128)} %param.10) | copy-start | bytes 393220
  89.3 132.0 %copy-start.2 = (bf16[128,8192]{1,0:T(8,128)(2,1)S(1)}, bf16[128,8192]{1,0:T(8,128)(2,1)}, u32[]{:S(2)}) copy-start(bf16[128,8192]{1,0:T(8,128)(2,1)} %param.11) | copy-start | bytes 6291460
  89.4 212.3 %all-gather.5.cloned.1.call-start = ((), (), s32[]{:S(2)}) async-start(), calls=%async_computation.7 | async-start | bytes 2162688 | tf_op jit(solution)/shard_map/all_gather | solution.py:32
  223.8 26.3 %all-to-all-start.2 = ((bf16[128,8,1024]{0,2,1:T(8,128)(2,1)}), bf16[128,8,1024]{0,2,1:T(8,128)(2,1)S(1)}, u32[]{:S(2)}, u32[]{:S(2)}) async-start(bf16[128,8,1024]{0,2,1:T(8,128)(2,1)} %bitcast.26), calls=%async_computation.3 | async-start | bytes 4194304 | tf_op jit(solution)/shard_map/all_to_all | solution.py:18
  250.1 1.3 copy-start.1
  251.4 56.1 %all-to-all-start = ((bf16[8,128,1024]{2,1,0:T(8,128)(2,1)}), bf16[8,128,1024]{2,1,0:T(8,128)(2,1)S(1)}, u32[]{:S(2)}, u32[]{:S(2)}) async-start(bf16[8,128,1024]{2,1,0:T(8,128)(2,1)} %bitcast.29), calls=%async_computation | async-start | bytes 4194304 | tf_op jit(solution)/shard_map/all_to_all | solution.py:27
  307.5 1.3 copy-start
  308.8 31.1 %all-to-all-start.3 = ((bf16[8,128,1024]{2,1,0:T(8,128)(2,1)}), bf16[8,128,1024]{2,1,0:T(8,128)(2,1)S(1)}, u32[]{:S(2)}, u32[]{:S(2)}) async-start(bf16[8,128,1024]{2,1,0:T(8,128)(2,1)} %bitcast.31), calls=%async_computation.4 | async-start | bytes 4194304 | tf_op jit(solution)/shard_map/all_to_all | solution.py:34
Sparse Core Ops, SparseCore 0:
  9.8 72.2 all-gather.2
  89.5 130.1 reduce-scatter.1
  223.4 78.1 all-gather.4
where the time goes:
time: 350 us; the launch traced here: 348 us
  waiting for transfers between devices  230 us (66%)
  blocking collectives  47.9 us (14%)
  matrix products  19 us (5%)
  local copies, waits for them, and re-layouts  18.8 us (5%)
  starting transfers between devices  15.7 us (4%)
  between operations  13.8 us (4%)
    reduce_scatter x1, waiting for transfers between devices, local(): lax.psum_scatter(inner_new, 'island', scatter_dimension=0, tiled=True)  130 us
    all_to_all x1, blocking collectives, local(): lax.all_to_all(activations, 'fsdp', split_axis=1, concat_axis=0, tiled=True)  47.9 us
    all_gather x1, waiting for transfers between devices, local(): island_block = lax.all_gather(new_share, 'island', axis=0, tiled=True)  41 us
    all_to_all x1, waiting for transfers between devices, local(): lax.all_to_all(partial.reshape(fsdp_count, tok_rows, -1), 'fsdp', split_a...  22.5 us
    all_gather x1, waiting for transfers between devices, local(): island_cotangent = lax.all_gather(cotangent, 'fsdp', axis=0, tiled=True)  19.7 us
    all_to_all x1, waiting for transfers between devices, local(): lax.all_to_all(next_activations, 'fsdp', split_axis=1, concat_axis=0, til...  15.6 us
    unnamed x12, local copies, waits for them, and re-layouts  9.17 us
    dot_general x1, matrix products, local(): lax.dot_general(column_block, island_cotangent, (((0,), (0,)), ((), ())),...  7.21 us
  transfers between devices with their start and end apart: 6, of which 5 were waited for; matrix products, arithmetic and copies ran while one was open for 8% of the time, Pallas kernels for 0%

commit v1 on v0

v1 whole, which is shorter than its diff:
```python
import functools

import jax
import jax.numpy as jnp
from jax import lax
from jax.experimental import pallas as pl
from jax.experimental.pallas import tpu as pltpu
from jax.sharding import PartitionSpec as P

inner_rate = 1.2
outer_rate = 0.7
nesterov = 0.9

TOK = 128
BLK = 1024
KV = 1024
SH = 32
F32 = jnp.float32
BF16 = jnp.bfloat16
MESH = pl.DeviceIdType.MESH


def kernel(x, g, w, ow, om, na, ig, nk, no, nm,
           wv, xr, gr, nar, igs, mine, tosib, fromsib, zs, zr, xs, xrv, nwb, ks, kr,
           loc, gss, grs, xss, xrs, nss, nrs, iss, irs, kss, krs, bss, brs, zss, zrs, hss, hrs, ass_, ars, axs, axr, sss, srs):
    isl = lax.axis_index("island")
    f = lax.axis_index("fsdp")
    core = isl % 2
    z = (isl // 2) % 8
    h = isl // 16
    yy = f // 2
    xl = f % 2

    def fdev(p):
        return {"island": isl, "fsdp": p}

    def peer(k):
        return ((yy + k // 2) % 4) * 2 + (xl + k % 2) % 2

    def source(k):
        return ((yy + 4 - k // 2) % 4) * 2 + (xl + k % 2) % 2

    sibling = {"island": h * 16 + z * 2 + 1 - core, "fsdp": f}
    partner = {"island": (1 - h) * 16 + z * 2 + core, "fsdp": f}
    zdev = [
        {"island": h * 16 + ((z + 1) % 8) * 2 + core, "fsdp": f},
        {"island": h * 16 + ((z + 7) % 8) * 2 + core, "fsdp": f},
    ]

    def cols(p):
        return pl.ds(pl.multiple_of(p * BLK, BLK), BLK)

    def rcopy(src, dst, ss, rs, dev):
        return pltpu.make_async_remote_copy(src_ref=src, dst_ref=dst, send_sem=ss, recv_sem=rs, device_id=dev, device_id_type=MESH)

    w_load = pltpu.make_async_copy(w.at[0], wv, loc.at[0])
    x_own = pltpu.make_async_copy(x.at[:, cols(f)], xr.at[f], loc.at[1])
    na_own = pltpu.make_async_copy(na.at[:, cols(f)], nar.at[f], loc.at[2])
    w_load.start()
    x_own.start()
    na_own.start()

    barrier = pltpu.get_barrier_semaphore()
    for k in range(1, 8):
        pl.semaphore_signal(barrier, inc=1, device_id=fdev(peer(k)), device_id_type=MESH)
    for dev in (sibling, partner, zdev[0], zdev[1]):
        pl.semaphore_signal(barrier, inc=1, device_id=dev, device_id_type=MESH)
    pl.semaphore_wait(barrier, 11)

    def g_copy(k):
        return rcopy(g, gr.at[f], gss.at[k], grs.at[k], fdev(peer(k)))

    def x_copy(k):
        return rcopy(x.at[:, cols(peer(k))], xr.at[f], xss.at[k], xrs.at[k], fdev(peer(k)))

    def na_copy(k):
        return rcopy(na.at[:, cols(peer(k))], nar.at[f], nss.at[k], nrs.at[k], fdev(peer(k)))

    def ig_copy(k):
        return rcopy(igs.at[source(k)], ig.at[:, cols(f)], iss.at[k], irs.at[k], fdev(source(k)))

    def key_copy(k):
        return rcopy(ks.at[source(k)], kr.at[f], kss.at[k], krs.at[k], fdev(source(k)))

    def each(body):
        lax.fori_loop(1, 8, lambda k, c: (body(k), c)[1], 0)

    each(lambda k: g_copy(k).start())
    each(lambda k: x_copy(k).start())
    each(lambda k: na_copy(k).start())
    gr[f] = g[...]

    w_load.wait()

    def grad_cols(s):
        igs[s] = lax.dot_general(gr[s], wv[...], (((1,), (1,)), ((), ())), preferred_element_type=F32).astype(BF16)

    def grad_step(k, c):
        @pl.when(k > 0)
        def _():
            g_copy(k).wait_recv()

        grad_cols(source(k))
        return c

    lax.fori_loop(0, 8, grad_step, 0)

    x_own.wait()
    each(lambda k: x_copy(k).wait_recv())

    def block_place(b):
        return b % 2, (z // 2 + 2 + b // 2) % 4

    def sib_copy(b):
        bh, bz = block_place(b)
        return rcopy(tosib.at[bh, pl.ds(bz * 2, 2)], fromsib.at[bh, pl.ds(bz * 2, 2)], bss.at[b], brs.at[b], sibling)

    def block_step(b, c):
        bh, bz = block_place(b)
        row = pl.multiple_of(bh * 512 + bz * 128, 128)
        xt = xr[:, :, pl.ds(row, 128)].reshape(8 * TOK, 128)
        grad = lax.dot_general(xt, gr[...].reshape(8 * TOK, KV), (((0,), (0,)), ((), ())), preferred_element_type=F32)
        new = wv[pl.ds(row, 128)].astype(F32) - inner_rate * (grad * (1.0 / 1024))
        new = new.reshape(2, 2, SH, KV)

        @pl.when(core == 0)
        def _():
            mine[bh, pl.ds(bz * 2, 2)] = new[:, 0]
            tosib[bh, pl.ds(bz * 2, 2)] = new[:, 1]

        @pl.when(core == 1)
        def _():
            mine[bh, pl.ds(bz * 2, 2)] = new[:, 1]
            tosib[bh, pl.ds(bz * 2, 2)] = new[:, 0]

        sib_copy(b).start()
        return c

    lax.fori_loop(0, 8, block_step, 0)
    for b in range(8):
        sib_copy(b).wait_recv()

    def z_copy(dirn, s, piece):
        return rcopy(zs.at[dirn, s, piece], zr.at[dirn, s, piece], zss.at[dirn, s, piece], zrs.at[dirn, s, piece], zdev[dirn])

    def used(dirn, s, piece):
        return s > 0 or piece == dirn

    for s in range(4):
        for piece in range(2):
            for dirn in range(2):
                if not used(dirn, s, piece):
                    continue
                t = (z + (4 - s if dirn == 0 else 4 + s)) % 8
                total = mine[piece, t] + fromsib[piece, t]
                if s > 0 and used(dirn, s - 1, piece):
                    z_copy(dirn, s - 1, piece).wait_recv()
                    total = total + zr[dirn, s - 1, piece].astype(F32)
                zs[dirn, s, piece] = total.astype(BF16)
                z_copy(dirn, s, piece).start()
    for piece in range(2):
        for dirn in range(2):
            z_copy(dirn, 3, piece).wait_recv()

    def z_total(piece):
        return mine[piece, z] + fromsib[piece, z] + zr[0, 3, piece].astype(F32) + zr[1, 3, piece].astype(F32)

    pair = rcopy(xs, xrv, hss, hrs, partner)
    xs[...] = z_total(1 - h)
    pair.start()
    own = z_total(h)
    pair.wait_recv()
    summed = own + xrv[...]
    pseudo = ow[...] - summed / 32
    momentum = nesterov * om[...] + pseudo
    outer = ow[...] - outer_rate * (pseudo + nesterov * momentum)
    nm[...] = momentum
    no[...] = outer

    def rows(ph, pz, pc):
        return pl.ds(pl.multiple_of(ph * 512 + pz * 64 + pc * 32, 32), SH)

    nwb[rows(h, z, core)] = outer.astype(BF16)

    def spread(ph, pz, ss, rs, dev):
        at = nwb.at[rows(ph, pz, core)]
        return rcopy(at, at, ss, rs, dev)

    def ring_copy(dirn, d, piece):
        pz = (z + (8 - d if dirn == 0 else d)) % 8
        return spread(piece, pz, ass_.at[dirn, d, piece], ars.at[dirn, d, piece], zdev[dirn])

    def ring_wait(dirn, d, piece):
        pz = (z + (7 - d if dirn == 0 else d + 1)) % 8
        return spread(piece, pz, ass_.at[dirn, d, piece], ars.at[dirn, d, piece], zdev[dirn]), pz

    def sib_spread(ph, pz):
        return spread(ph, pz, sss.at[ph, pz], srs.at[ph, pz], sibling)

    cross = spread(h, z, axs, axr, partner)
    cross.start()
    for dirn in range(2):
        rcopy(nwb.at[rows(h, z, core)], nwb.at[rows(h, z, core)], ass_.at[dirn, 0, h], ars.at[dirn, 0, h], zdev[dirn]).start()
    sib_spread(h, z).start()
    each(lambda k: ig_copy(k).start())
    ig_own = pltpu.make_async_copy(igs.at[f], ig.at[:, cols(f)], loc.at[3])
    ig_own.start()
    cross.wait_recv()
    for dirn in range(2):
        rcopy(nwb.at[rows(1 - h, z, core)], nwb.at[rows(1 - h, z, core)], ass_.at[dirn, 0, 1 - h], ars.at[dirn, 0, 1 - h], zdev[dirn]).start()
    sib_spread(1 - h, z).start()
    for d in range(4):
        for piece in range(2):
            for dirn in range(2):
                if d == 3 and piece != dirn:
                    continue
                arrival, pz = ring_wait(dirn, d, piece)
                arrival.wait_recv()
                last = 3 if piece == dirn else 2
                if d < last:
                    ring_copy(dirn, d + 1, piece).start()
                sib_spread(piece, pz).start()

    na_own.wait()
    each(lambda k: na_copy(k).wait_recv())
    for ph in range(2):
        for pz in range(8):
            at = nwb.at[rows(ph, pz, 1 - core)]
            rcopy(at, at, sss.at[ph, pz], srs.at[ph, pz], sibling).wait_recv()

    def key_step(k, c):
        s = source(k)
        ks[s] = jnp.dot(nar[s], nwb[...], preferred_element_type=F32).astype(BF16)
        key_copy(k).start()
        return c

    lax.fori_loop(1, 8, key_step, 0)
    keys = jnp.dot(nar[f], nwb[...], preferred_element_type=F32)
    each(lambda k: key_copy(k).wait_recv())
    nk[...] = keys

    def add_step(k, c):
        nk[...] += kr[peer(k)].astype(F32)
        return c

    lax.fori_loop(1, 8, add_step, 0)

    each(lambda k: ig_copy(k).wait_recv())
    ig_own.wait()
    for copy_of in (g_copy, x_copy, na_copy, ig_copy, key_copy):
        each(lambda k: copy_of(k).wait_send())
    for b in range(8):
        sib_copy(b).wait_send()
    for s in range(4):
        for piece in range(2):
            for dirn in range(2):
                if used(dirn, s, piece):
                    z_copy(dirn, s, piece).wait_send()
    pair.wait_send()
    cross.wait_send()
    for d in range(4):
        for piece in range(2):
            for dirn in range(2):
                if d < 3 or piece == dirn:
                    ring_copy(dirn, d, piece).wait_send()
    for ph in range(2):
        for pz in range(8):
            sib_spread(ph, pz).wait_send()


def local(activations, cotangent, inner_weight, outer_weight, outer_momentum, next_activations):
    vm = pl.BlockSpec(memory_space=pltpu.VMEM)
    hb = pl.BlockSpec(memory_space=pl.ANY)
    dma = pltpu.SemaphoreType.DMA
    ig, nk, no, nm = pl.pallas_call(
        kernel,
        out_shape=(
            jax.ShapeDtypeStruct((TOK, 8 * BLK), BF16),
            jax.ShapeDtypeStruct((TOK, KV), F32),
            jax.ShapeDtypeStruct((SH, KV), F32),
            jax.ShapeDtypeStruct((SH, KV), F32),
        ),
        in_specs=[hb, vm, hb, vm, vm, hb],
        out_specs=(hb, vm, vm, vm),
        scratch_shapes=[
            pltpu.VMEM((BLK, KV), BF16),
            pltpu.VMEM((8, TOK, BLK), BF16),
            pltpu.VMEM((8, TOK, KV), BF16),
            pltpu.VMEM((8, TOK, BLK), BF16),
            pltpu.VMEM((8, TOK, BLK), BF16),
            pltpu.VMEM((2, 8, SH, KV), F32),
            pltpu.VMEM((2, 8, SH, KV), F32),
            pltpu.VMEM((2, 8, SH, KV), F32),
            pltpu.VMEM((2, 4, 2, SH, KV), BF16),
            pltpu.VMEM((2, 4, 2, SH, KV), BF16),
            pltpu.VMEM((SH, KV), F32),
            pltpu.VMEM((SH, KV), F32),
            pltpu.VMEM((BLK, KV), BF16),
            pltpu.VMEM((8, TOK, KV), BF16),
            pltpu.VMEM((8, TOK, KV), BF16),
            dma((4,)),
            dma((8,)), dma((8,)),
            dma((8,)), dma((8,)),
            dma((8,)), dma((8,)),
            dma((8,)), dma((8,)),
            dma((8,)), dma((8,)),
            dma((8,)), dma((8,)),
            dma((2, 4, 2)), dma((2, 4, 2)),
            dma, dma,
            dma((2, 4, 2)), dma((2, 4, 2)),
            dma, dma,
            dma((2, 8)), dma((2, 8)),
        ],
        compiler_params=pltpu.CompilerParams(collective_id=0, has_side_effects=True, vmem_limit_bytes=60 * 1024 * 1024),
    )(activations, cotangent, inner_weight, outer_weight, outer_momentum, next_activations)
    return ig, nk.astype(BF16), no, nm


def solution(mesh):
    in_specs = (
        P(("island", "fsdp"), None),
        P(("island", "fsdp"), None),
        P("island", "fsdp", None),
        P(("fsdp", "island"), None),
        P(("fsdp", "island"), None),
        P(("island", "fsdp"), None),
    )
    out_specs = (
        P(("island", "fsdp"), None),
        P(("island", "fsdp"), None),
        P(("fsdp", "island"), None),
        P(("fsdp", "island"), None),
    )
    return jax.shard_map(local, mesh=mesh, in_specs=in_specs, out_specs=out_specs, check_vma=False)
```

time: 350 us -> 144 us (0.41)
  waiting for transfers between devices: 230 us -> 0 us
  Pallas kernels: 0 us -> 135 us
  blocking collectives: 47.9 us -> 0 us
  matrix products: 19 us -> 0 us
  starting transfers between devices: 15.7 us -> 0 us
  local copies, waits for them, and re-layouts: 18.8 us -> 4.46 us
  between operations: 13.8 us -> 0.64 us
    pallas_call x0 -> x1, Pallas kernels: none -> 135 us  [local(): pl.pallas_call(kernel, out_shape=(jax.ShapeDtypeStruct((TOK, 8 * BLK), BF...]
    reduce_scatter x1 -> x0, waiting for transfers between devices: 130 us -> none  [local(): lax.psum_scatter(inner_new, 'island', scatter_dimension=0, tiled=True)]
    all_gather x2 -> x0, waiting for transfers between devices: 60.6 us -> none  [the longest x1 41 us: local(): island_block = lax.all_gather(new_share, 'island', axis=0, tiled=True)]
    all_to_all x1 -> x0, blocking collectives: 47.9 us -> none  [local(): lax.all_to_all(activations, 'fsdp', split_axis=1, concat_axis=0, tiled=True)]
    all_to_all x3 -> x0, waiting for transfers between devices: 38.1 us -> none  [the longest x1 22.5 us: local(): lax.all_to_all(partial.reshape(fsdp_count, tok_rows, -1), 'fsdp', split_a...]
    dot_general x3 -> x0, matrix products: 19 us -> none  [the longest x1 7.21 us: local(): lax.dot_general(column_block, island_cotangent, (((0,), (0,)), ((), ())),...]
    all_to_all x3 -> x0, starting transfers between devices: 15.6 us -> none  [the longest x1 5.51 us: local(): lax.all_to_all(partial.reshape(fsdp_count, tok_rows, -1), 'fsdp', split_a...]
    all_to_all x3 -> x0, local copies, waits for them, and re-layouts: 9.65 us -> none  [the longest x1 3.92 us: local(): lax.all_to_all(next_activations, 'fsdp', split_axis=1, concat_axis=0, til...]
  transfers between devices with their start and end apart: 6 -> 0, of which waited for: 5 -> 0; matrix products, arithmetic and copies ran while one was open for 8% -> 0% of each run, Pallas kernels for 0% -> 0%
where the time goes in v1:
time: 144 us; the launch traced here: 142 us
  Pallas kernels  135 us (94%)
  local copies, waits for them, and re-layouts  4.46 us (3%)
  other arithmetic  1.78 us (1%)
    pallas_call x1, Pallas kernels, local(): pl.pallas_call(kernel, out_shape=(jax.ShapeDtypeStruct((TOK, 8 * BLK), BF...  135 us
    unnamed x7, local copies, waits for them, and re-layouts  4.46 us

profile of v1, /device:TPU:8, one launch (start us, length us, event | category | flops | bytes accessed | tf_op | source)
XLA Modules:
  0.0 141.7 jit_solution(785465723782338371)
XLA Ops:
  0.6 134.8 %shard_map.93 = (bf16[128,8192]{1,0:T(8,128)(2,1)}, f32[128,1024]{1,0:T(8,128)}, f32[32,1024]{1,0:T(8,128)}, f32[32,1024]{1,0:T(8,128)}) custom-call(bf16[128,8192]{1,0:T(8,128)(2,1)} %x.1, bf16[128,1024]{1,0:T(8,128)(2,1)} %g.1, bf16[1,1024,1024]{2,1,0:T(8,128)(2,1)} %w.1, f32[32,1024]{1,0:T(8,128)} %ow.1, f32[32,1024]{1,0:T(8,128)} %om.1, bf16[128,8192]{1,0:T(8,128)(2,1)} %na.1), custom_call_target="tpu_custom_call" | custom-call | tf_op jit(solution)/shard_map/pallas_call | solution.py:275
  135.4 1.8 %convert_element_type.3 = bf16[128,1024]{1,0:T(8,128)(2,1)} convert(f32[128,1024]{1,0:T(8,128)} %get-tuple-element.9) | non-fusion elementwise | flops 131072 | bytes 786432 | tf_op jit(solution)/shard_map/convert_element_type | solution.py:316
  137.2 0.0 copy-start.1
  137.2 0.0 copy-start
  137.2 3.1 %copy.13 = bf16[128,8192]{1,0:T(8,128)(2,1)} copy(bf16[128,8192]{1,0:T(8,128)(2,1)} %get-tuple-element.16) | data formatting | bytes 4194304
  140.4 0.0 copy-done.1
  140.4 0.7 copy.14
  141.0 0.0 copy-done
  141.0 0.7 copy.15
Async XLA Ops:
  137.2 3.1 %copy-start.1 = (f32[32,1024]{1,0:T(8,128)S(1)}, f32[32,1024]{1,0:T(8,128)}, u32[]{:S(2)}) copy-start(f32[32,1024]{1,0:T(8,128)} %get-tuple-element.18) | copy-start | bytes 393220
  137.2 3.8 %copy-start = (f32[32,1024]{1,0:T(8,128)S(1)}, f32[32,1024]{1,0:T(8,128)}, u32[]{:S(2)}) copy-start(f32[32,1024]{1,0:T(8,128)} %get-tuple-element.19) | copy-start | bytes 393220

commit v2 on v1

v2 whole, which is shorter than its diff:
```python
import functools

import jax
import jax.numpy as jnp
from jax import lax
from jax.experimental import pallas as pl
from jax.experimental.pallas import tpu as pltpu
from jax.sharding import PartitionSpec as P

inner_rate = 1.2
outer_rate = 0.7
nesterov = 0.9

TOK = 128
BLK = 1024
KV = 1024
SH = 32
HALF = 512
F32 = jnp.float32
BF16 = jnp.bfloat16
MESH = pl.DeviceIdType.MESH


def kernel(x, g, w, ow, om, na, ig, nk, no, nm,
           wv, xr, gr, glo, nar, igs, mine, tosib, fromsib, zs, zr, xs, xrv, nw, ksx, krx, ksy, kry, acc,
           loc, gys, gyr, gxs, gxr, xss, xrs, nss, nrs, iss, irs, kxs, kxr, kys, kyr, bss, brs, zss, zrs, hss, hrs,
           ass_, ars, axs, axr, sss, srs):
    isl = lax.axis_index("island")
    f = lax.axis_index("fsdp")
    core = isl % 2
    z = (isl // 2) % 8
    h = isl // 16
    yy = f // 2
    xl = f % 2
    across = (1 - h) * 16 + z * 2 + core

    def same(dy):
        return {"island": isl, "fsdp": ((yy + dy) % 4) * 2 + xl}

    def low(dy):
        return {"island": isl, "fsdp": ((yy + dy) % 4) * 2 + 1 - xl}

    def high(dy):
        return {"island": across, "fsdp": ((yy + dy) % 4) * 2 + 1 - xl}

    sibling = {"island": h * 16 + z * 2 + 1 - core, "fsdp": f}
    partner = {"island": across, "fsdp": f}
    zdev = [
        {"island": h * 16 + ((z + 1) % 8) * 2 + core, "fsdp": f},
        {"island": h * 16 + ((z + 7) % 8) * 2 + core, "fsdp": f},
    ]
    routes = [(same(dy), 0, TOK, yy * TOK) for dy in (1, 3, 2)]
    routes += [(low(dy), 0, 64, 512 + yy * 64) for dy in range(4)]
    routes += [(high(dy), 64, 64, 768 + yy * 64) for dy in range(4)]

    def at_rows(start, size, step):
        return pl.ds(pl.multiple_of(start, step), size)

    def cols(p):
        return at_rows(p * BLK, BLK, BLK)

    def rcopy(src, dst, ss, rs, dev):
        return pltpu.make_async_remote_copy(src_ref=src, dst_ref=dst, send_sem=ss, recv_sem=rs, device_id=dev, device_id_type=MESH)

    w_load = pltpu.make_async_copy(w.at[0], wv, loc.at[0])
    own = [pltpu.make_async_copy(x.at[:, cols(f)], xr.at[at_rows(yy * TOK, TOK, TOK)], loc.at[1]),
           pltpu.make_async_copy(na.at[:, cols(f)], nar.at[at_rows(yy * TOK, TOK, TOK)], loc.at[2])]
    w_load.start()
    own[0].start()
    own[1].start()

    barrier = pltpu.get_barrier_semaphore()
    for dev in [r[0] for r in routes] + [sibling, partner, zdev[0], zdev[1]]:
        pl.semaphore_signal(barrier, inc=1, device_id=dev, device_id_type=MESH)
    pl.semaphore_wait(barrier, 15)

    def gy_copy(n):
        return rcopy(g, gr.at[at_rows(yy * TOK, TOK, TOK)], gys.at[n], gyr.at[n], routes[n][0])

    def gx_copy(n, y):
        src = gr.at[at_rows(y * TOK + (0 if n == 0 else 64), 64, 64)]
        if n == 2:
            dst = glo.at[at_rows(y * 64, 64, 64)]
        else:
            dst = gr.at[at_rows(512 + n * 256 + y * 64, 64, 64)]
        return rcopy(src, dst, gxs.at[n, y], gxr.at[n, y], high(0) if n == 1 else low(0))

    def block_place(b):
        group = b // 2
        return b % 2, (z // 2 + (2 + group * 3 + (group // 2) * 3 + (group // 3) * 2)) % 4

    def x_copy(b, n):
        bh, bz = block_place(b)
        row = bh * 512 + bz * 128
        dev, first, size, to = routes[n]
        src = x.at[pl.ds(first, size), at_rows(dev["fsdp"] * BLK + row, 128, 128)]
        return rcopy(src, xr.at[at_rows(to, size, size), at_rows(row, 128, 128)], xss.at[b, n], xrs.at[b, n], dev)

    def na_copy(n):
        dev, first, size, to = routes[n]
        return rcopy(na.at[pl.ds(first, size), cols(dev["fsdp"])], nar.at[at_rows(to, size, size)], nss.at[n], nrs.at[n], dev)

    def ig_copy(n):
        if n < 3:
            dy = (1, 3, 2)[n]
            src, rows, dev = igs.at[at_rows(((yy + dy) % 4) * TOK, TOK, TOK)], pl.ds(0, TOK), same(dy)
        else:
            dy, half = (n - 3) % 4, (n - 3) // 4
            src, rows, dev = igs.at[at_rows(512 + half * 256 + ((yy + dy) % 4) * 64, 64, 64)], pl.ds(half * 64, 64), low(dy)
        return rcopy(src, ig.at[rows, cols(f)], iss.at[n], irs.at[n], dev)

    def send_x(b, c):
        for n in range(11):
            x_copy(b, n).start()
        return c

    for n in range(3):
        gy_copy(n).start()
    gr[at_rows(yy * TOK, TOK, TOK)] = g[...]
    for n in range(2):
        rcopy(g.at[pl.ds(n * 64, 64)], gr.at[at_rows(512 + n * 256 + yy * 64, 64, 64)], gxs.at[n, yy], gxr.at[n, yy],
              high(0) if n == 1 else low(0)).start()
    lax.fori_loop(0, 2, send_x, 0)
    for n, dy in enumerate((1, 3, 2)):
        gy_copy(n).wait_recv()
        for m in range(2):
            gx_copy(m, (yy + 4 - dy) % 4).start()
    lax.fori_loop(2, 8, send_x, 0)
    rcopy(g.at[pl.ds(64, 64)], glo.at[at_rows(yy * 64, 64, 64)], gxs.at[2, yy], gxr.at[2, yy], low(0)).start()
    for dy in (1, 3, 2):
        gx_copy(2, (yy + 4 - dy) % 4).start()

    w_load.wait()

    def grad_cols(values):
        return lax.dot_general(values, wv[...], (((1,), (1,)), ((), ())), preferred_element_type=F32).astype(BF16)

    def grad_step(k, c):
        rows = at_rows(k * TOK, TOK, TOK)
        igs[rows] = grad_cols(gr[rows])
        return c

    lax.fori_loop(0, 4, grad_step, 0)
    for m in range(2):
        for y in range(4):
            gx_copy(m, y).wait_recv()
    lax.fori_loop(4, 6, grad_step, 0)
    for n in range(3):
        na_copy(n).start()
    for n in range(3, 7):
        ig_copy(n).start()

    own[0].wait()

    def sib_copy(b):
        bh, bz = block_place(b)
        return rcopy(tosib.at[bh, pl.ds(bz * 2, 2)], fromsib.at[bh, pl.ds(bz * 2, 2)], bss.at[b], brs.at[b], sibling)

    def block_step(b, c):
        for n in range(11):
            x_copy(b, n).wait_recv()
        bh, bz = block_place(b)
        row = at_rows(bh * 512 + bz * 128, 128, 128)
        grad = lax.dot_general(xr[:, row], gr[...], (((0,), (0,)), ((), ())), preferred_element_type=F32)
        new = wv[row].astype(F32) - inner_rate * (grad * (1.0 / 1024))
        new = new.reshape(2, 2, SH, KV)

        @pl.when(core == 0)
        def _():
            mine[bh, pl.ds(bz * 2, 2)] = new[:, 0]
            tosib[bh, pl.ds(bz * 2, 2)] = new[:, 1]

        @pl.when(core == 1)
        def _():
            mine[bh, pl.ds(bz * 2, 2)] = new[:, 1]
            tosib[bh, pl.ds(bz * 2, 2)] = new[:, 0]

        sib_copy(b).start()
        return c

    def z_copy(dirn, s, piece):
        return rcopy(zs.at[dirn, s, piece], zr.at[dirn, s, piece], zss.at[dirn, s, piece], zrs.at[dirn, s, piece], zdev[dirn])

    def used(dirn, s, piece):
        return s > 0 or piece == dirn

    def ring_step(s, dirns):
        for piece in range(2):
            for dirn in dirns:
                if not used(dirn, s, piece):
                    continue
                t = (z + (4 - s if dirn == 0 else 4 + s)) % 8
                total = mine[piece, t] + fromsib[piece, t]
                if s > 0 and used(dirn, s - 1, piece):
                    z_copy(dirn, s - 1, piece).wait_recv()
                    total = total + zr[dirn, s - 1, piece].astype(F32)
                zs[dirn, s, piece] = total.astype(BF16)
                z_copy(dirn, s, piece).start()

    for group in range(4):
        lax.fori_loop(2 * group, 2 * group + 2, block_step, 0)
        for b in (2 * group, 2 * group + 1):
            sib_copy(b).wait_recv()
        if group == 0:
            ring_step(0, (0, 1))
        elif group == 1:
            ring_step(1, (0,))
        elif group == 2:
            ring_step(1, (1,))
            ring_step(2, (0, 1))
        else:
            ring_step(3, (0, 1))
    for piece in range(2):
        for dirn in range(2):
            z_copy(dirn, 3, piece).wait_recv()

    def z_total(piece):
        return mine[piece, z] + fromsib[piece, z] + zr[0, 3, piece].astype(F32) + zr[1, 3, piece].astype(F32)

    pair = rcopy(xs, xrv, hss, hrs, partner)
    xs[...] = z_total(1 - h)
    pair.start()
    own_sum = z_total(h)
    pair.wait_recv()
    summed = own_sum + xrv[...]
    pseudo = ow[...] - summed / 32
    momentum = nesterov * om[...] + pseudo
    outer = ow[...] - outer_rate * (pseudo + nesterov * momentum)
    nm[...] = momentum
    no[...] = outer

    share = outer.astype(BF16)
    for part in range(2):
        nw[part, h, z, core] = share[:, part * HALF:(part + 1) * HALF]

    def spread(part, ph, pz, ss, rs, dev):
        at = nw.at[part, ph, pz, core]
        return rcopy(at, at, ss, rs, dev)

    def ring_copy(part, dirn, d, piece):
        pz = (z + (8 - d if dirn == 0 else d)) % 8
        return spread(part, piece, pz, ass_.at[part, dirn, d, piece], ars.at[part, dirn, d, piece], zdev[dirn])

    def ring_first(part, ph):
        for dirn in range(2):
            spread(part, ph, z, ass_.at[part, dirn, 0, ph], ars.at[part, dirn, 0, ph], zdev[dirn]).start()

    def sib_spread(part, ph, pz):
        return spread(part, ph, pz, sss.at[part, ph, pz], srs.at[part, ph, pz], sibling)

    def cross(part):
        return spread(part, h, z, axs.at[part], axr.at[part], partner)

    for part in range(2):
        cross(part).start()
    for part in range(2):
        ring_first(part, h)
        sib_spread(part, h, z).start()
    for n in range(3, 11):
        na_copy(n).start()
    for part in range(2):
        cross(part).wait_recv()
        ring_first(part, 1 - h)
        sib_spread(part, 1 - h, z).start()
    for n in range(3):
        ig_copy(n).start()
    for y in range(4):
        gx_copy(2, y).wait_recv()

    def late_step(k, c):
        igs[at_rows(768 + k * TOK, TOK, TOK)] = grad_cols(glo[at_rows(k * TOK, TOK, TOK)])
        return c

    lax.fori_loop(0, 2, late_step, 0)
    for n in range(7, 9):
        ig_copy(n).start()
    ig_own = pltpu.make_async_copy(igs.at[at_rows(yy * TOK, TOK, TOK)], ig.at[:, cols(f)], loc.at[3])
    ig_own.start()

    def ring_arrival(part, d):
        for piece in range(2):
            for dirn in range(2):
                if d == 3 and piece != dirn:
                    continue
                ring_copy(part, dirn, d, piece).wait_recv()
                if d < (3 if piece == dirn else 2):
                    ring_copy(part, dirn, d + 1, piece).start()
                sib_spread(part, piece, (z + (7 - d if dirn == 0 else d + 1)) % 8).start()

    for d in range(4):
        for part in range(2):
            ring_arrival(part, d)

    def kx_copy(part, side):
        return rcopy(ksx.at[part, side], krx.at[part, side], kxs.at[part, side], kxr.at[part, side], high(0) if side else low(0))

    def ky_copy(part, n):
        dy = (1, 3, 2)[n]
        return rcopy(ksy.at[part, (yy + dy) % 4], kry.at[part, yy], kys.at[part, n], kyr.at[part, n], same(dy))

    own[1].wait()
    for n in range(11):
        na_copy(n).wait_recv()
    for part in range(2):
        for ph in range(2):
            for pz in range(8):
                sib_spread(part, ph, pz).wait_recv()
        for side in range(2):
            rows = pl.ds(512 + side * 256, 256)
            ksx[part, side] = jnp.dot(nar[rows], nw[part].reshape(BLK, HALF), preferred_element_type=F32).astype(BF16)
            kx_copy(part, side).start()
    for n in range(9, 11):
        ig_copy(n).start()
    for part in range(2):
        def own_step(y, c):
            acc[part, y] = jnp.dot(nar[at_rows(y * TOK, TOK, TOK)], nw[part].reshape(BLK, HALF), preferred_element_type=F32)
            return c

        lax.fori_loop(0, 4, own_step, 0)
    for part in range(2):
        for side in range(2):
            kx_copy(part, side).wait_recv()

        def pair_sum(y):
            other = jnp.concatenate([krx[part, 0, at_rows(y * 64, 64, 64)], krx[part, 1, at_rows(y * 64, 64, 64)]], axis=0)
            return acc[part, y] + other.astype(F32)

        for n in range(3):
            to = (yy + (1, 3, 2)[n]) % 4
            ksy[part, to] = pair_sum(to).astype(BF16)
            ky_copy(part, n).start()
        acc[part, yy] = pair_sum(yy)
    for part in range(2):
        total = acc[part, yy]
        for n in range(3):
            ky_copy(part, n).wait_recv()
            total = total + kry[part, (yy + 4 - (1, 3, 2)[n]) % 4].astype(F32)
        nk[:, pl.ds(part * HALF, HALF)] = total.astype(BF16)

    for n in range(11):
        ig_copy(n).wait_recv()
    ig_own.wait()
    for n in range(11):
        ig_copy(n).wait_send()
        na_copy(n).wait_send()
    for n in range(3):
        gy_copy(n).wait_send()
        for y in range(4):
            gx_copy(n, y).wait_send()

    def drain_x(b, c):
        for n in range(11):
            x_copy(b, n).wait_send()
        return c

    lax.fori_loop(0, 8, drain_x, 0)
    for b in range(8):
        sib_copy(b).wait_send()
    for s in range(4):
        for piece in range(2):
            for dirn in range(2):
                if used(dirn, s, piece):
                    z_copy(dirn, s, piece).wait_send()
    pair.wait_send()
    for part in range(2):
        cross(part).wait_send()
        for d in range(4):
            for piece in range(2):
                for dirn in range(2):
                    if d < 3 or piece == dirn:
                        ring_copy(part, dirn, d, piece).wait_send()
        for ph in range(2):
            for pz in range(8):
                sib_spread(part, ph, pz).wait_send()
        for side in range(2):
            kx_copy(part, side).wait_send()
        for n in range(3):
            ky_copy(part, n).wait_send()


def local(activations, cotangent, inner_weight, outer_weight, outer_momentum, next_activations):
    vm = pl.BlockSpec(memory_space=pltpu.VMEM)
    hb = pl.BlockSpec(memory_space=pl.ANY)
    dma = pltpu.SemaphoreType.DMA
    ig, nk, no, nm = pl.pallas_call(
        kernel,
        out_shape=(
            jax.ShapeDtypeStruct((TOK, 8 * BLK), BF16),
            jax.ShapeDtypeStruct((TOK, KV), BF16),
            jax.ShapeDtypeStruct((SH, KV), F32),
            jax.ShapeDtypeStruct((SH, KV), F32),
        ),
        in_specs=[hb, vm, hb, vm, vm, hb],
        out_specs=(hb, vm, vm, vm),
        scratch_shapes=[
            pltpu.VMEM((BLK, KV), BF16),
            pltpu.VMEM((8 * TOK, BLK), BF16),
            pltpu.VMEM((8 * TOK, KV), BF16),
            pltpu.VMEM((256, KV), BF16),
            pltpu.VMEM((8 * TOK, BLK), BF16),
            pltpu.VMEM((8 * TOK, BLK), BF16),
            pltpu.VMEM((2, 8, SH, KV), F32),
            pltpu.VMEM((2, 8, SH, KV), F32),
            pltpu.VMEM((2, 8, SH, KV), F32),
            pltpu.VMEM((2, 4, 2, SH, KV), BF16),
            pltpu.VMEM((2, 4, 2, SH, KV), BF16),
            pltpu.VMEM((SH, KV), F32),
            pltpu.VMEM((SH, KV), F32),
            pltpu.VMEM((2, 2, 8, 2, SH, HALF), BF16),
            pltpu.VMEM((2, 2, 256, HALF), BF16),
            pltpu.VMEM((2, 2, 256, HALF), BF16),
            pltpu.VMEM((2, 4, TOK, HALF), BF16),
            pltpu.VMEM((2, 4, TOK, HALF), BF16),
            pltpu.VMEM((2, 4, TOK, HALF), F32),
            dma((4,)),
            dma((3,)), dma((3,)),
            dma((3, 4)), dma((3, 4)),
            dma((8, 11)), dma((8, 11)),
            dma((11,)), dma((11,)),
            dma((11,)), dma((11,)),
            dma((2, 2)), dma((2, 2)),
            dma((2, 3)), dma((2, 3)),
            dma((8,)), dma((8,)),
            dma((2, 4, 2)), dma((2, 4, 2)),
            dma, dma,
            dma((2, 2, 4, 2)), dma((2, 2, 4, 2)),
            dma((2,)), dma((2,)),
            dma((2, 2, 8)), dma((2, 2, 8)),
        ],
        compiler_params=pltpu.CompilerParams(collective_id=0, has_side_effects=True, vmem_limit_bytes=60 * 1024 * 1024),
    )(activations, cotangent, inner_weight, outer_weight, outer_momentum, next_activations)
    return ig, nk, no, nm


def solution(mesh):
    in_specs = (
        P(("island", "fsdp"), None),
        P(("island", "fsdp"), None),
        P("island", "fsdp", None),
        P(("fsdp", "island"), None),
        P(("fsdp", "island"), None),
        P(("island", "fsdp"), None),
    )
    out_specs = (
        P(("island", "fsdp"), None),
        P(("island", "fsdp"), None),
        P(("fsdp", "island"), None),
        P(("fsdp", "island"), None),
    )
    return jax.shard_map(local, mesh=mesh, in_specs=in_specs, out_specs=out_specs, check_vma=False)
```

time: 144 us -> 126 us (0.88); the launches traced: 142 us -> 126 us
  Pallas kernels: 135 us -> 121 us
  other arithmetic: 1.78 us -> 0 us
    pallas_call x1, Pallas kernels: 135 us -> 121 us  [local(): pl.pallas_call(kernel, out_shape=(jax.ShapeDtypeStruct((TOK, 8 * BLK), BF...]
    convert_element_type x1 -> x0, other arithmetic: 1.78 us -> none  [local(): return (ig, nk.astype(BF16), no, nm)]
    unnamed x7 -> x10, local copies, waits for them, and re-layouts: 4.46 us -> 5.17 us
where the time goes in v2:
time: 126 us
  Pallas kernels  121 us (96%)
  local copies, waits for them, and re-layouts  5.17 us (4%)
    pallas_call x1, Pallas kernels, local(): pl.pallas_call(kernel, out_shape=(jax.ShapeDtypeStruct((TOK, 8 * BLK), BF...  121 us
    unnamed x10, local copies, waits for them, and re-layouts  5.17 us

profile of v2, /device:TPU:8, one launch (start us, length us, event | category | flops | bytes accessed | tf_op | source)
XLA Modules:
  0.0 126.4 jit_solution(13065995842257612581)
XLA Ops:
  0.6 120.5 %shard_map.93 = (bf16[128,8192]{1,0:T(8,128)(2,1)}, bf16[128,1024]{1,0:T(8,128)(2,1)}, f32[32,1024]{1,0:T(8,128)}, f32[32,1024]{1,0:T(8,128)}) custom-call(bf16[128,8192]{1,0:T(8,128)(2,1)} %x.1, bf16[128,1024]{1,0:T(8,128)(2,1)} %g.1, bf16[1,1024,1024]{2,1,0:T(8,128)(2,1)} %w.1, f32[32,1024]{1,0:T(8,128)} %ow.1, f32[32,1024]{1,0:T(8,128)} %om.1, ...), custom_call_target="tpu_custom_call" | custom-call | tf_op jit(solution)/shard_map/pallas_call | solution.py:385
  121.2 0.0 copy-start
  121.2 0.0 copy-start.2
  121.2 0.0 copy-start.1
  121.2 3.1 %copy.14 = bf16[128,8192]{1,0:T(8,128)(2,1)} copy(bf16[128,8192]{1,0:T(8,128)(2,1)} %get-tuple-element.8) | data formatting | bytes 4194304
  124.3 0.0 copy-done
  124.3 0.7 copy.15
  125.0 0.0 copy-done.2
  125.0 0.7 copy.16
  125.7 0.0 copy-done.1
  125.7 0.7 copy.17
Async XLA Ops:
  121.2 3.2 %copy-start = (bf16[128,1024]{1,0:T(8,128)(2,1)S(1)}, bf16[128,1024]{1,0:T(8,128)(2,1)}, u32[]{:S(2)}) copy-start(bf16[128,1024]{1,0:T(8,128)(2,1)} %get-tuple-element.9) | copy-start | bytes 786436
  121.2 3.9 %copy-start.2 = (f32[32,1024]{1,0:T(8,128)S(1)}, f32[32,1024]{1,0:T(8,128)}, u32[]{:S(2)}) copy-start(f32[32,1024]{1,0:T(8,128)} %get-tuple-element.10) | copy-start | bytes 393220
  121.2 4.5 %copy-start.1 = (f32[32,1024]{1,0:T(8,128)S(1)}, f32[32,1024]{1,0:T(8,128)}, u32[]{:S(2)}) copy-start(f32[32,1024]{1,0:T(8,128)} %get-tuple-element.11) | copy-start | bytes 393220

commit v3 on v2

--- a/solution.py
+++ b/solution.py
@@ -16,6 +16,8 @@
 KV = 1024
 SH = 32
 HALF = 512
+QUAD = 256
+XEARLY = 4
 F32 = jnp.float32
 BF16 = jnp.bfloat16
 MESH = pl.DeviceIdType.MESH
@@ -87,10 +89,12 @@
 
     def block_place(b):
         group = b // 2
-        return b % 2, (z // 2 + (2 + group * 3 + (group // 2) * 3 + (group // 3) * 2)) % 4
+        return (1 - h + b) % 2, (z // 2 + (2 + group * 3 + (group // 2) * 3 + (group // 3) * 2)) % 4
 
     def x_copy(b, n):
         bh, bz = block_place(b)
+        if n >= 7:
+            bh = 1 - bh
         row = bh * 512 + bz * 128
         dev, first, size, to = routes[n]
         src = x.at[pl.ds(first, size), at_rows(dev["fsdp"] * BLK + row, 128, 128)]
@@ -109,10 +113,13 @@
             src, rows, dev = igs.at[at_rows(512 + half * 256 + ((yy + dy) % 4) * 64, 64, 64)], pl.ds(half * 64, 64), low(dy)
         return rcopy(src, ig.at[rows, cols(f)], iss.at[n], irs.at[n], dev)
 
-    def send_x(b, c):
-        for n in range(11):
-            x_copy(b, n).start()
-        return c
+    def send_x(routed):
+        def body(b, c):
+            for n in routed:
+                x_copy(b, n).start()
+            return c
+
+        return body
 
     for n in range(3):
         gy_copy(n).start()
@@ -120,12 +127,13 @@
     for n in range(2):
         rcopy(g.at[pl.ds(n * 64, 64)], gr.at[at_rows(512 + n * 256 + yy * 64, 64, 64)], gxs.at[n, yy], gxr.at[n, yy],
               high(0) if n == 1 else low(0)).start()
-    lax.fori_loop(0, 2, send_x, 0)
+    lax.fori_loop(0, XEARLY, send_x(range(3)), 0)
     for n, dy in enumerate((1, 3, 2)):
         gy_copy(n).wait_recv()
         for m in range(2):
             gx_copy(m, (yy + 4 - dy) % 4).start()
-    lax.fori_loop(2, 8, send_x, 0)
+    lax.fori_loop(0, XEARLY, send_x(range(3, 11)), 0)
+    lax.fori_loop(XEARLY, 8, send_x(range(11)), 0)
     rcopy(g.at[pl.ds(64, 64)], glo.at[at_rows(yy * 64, 64, 64)], gxs.at[2, yy], gxr.at[2, yy], low(0)).start()
     for dy in (1, 3, 2):
         gx_copy(2, (yy + 4 - dy) % 4).start()
@@ -184,43 +192,41 @@
     def used(dirn, s, piece):
         return s > 0 or piece == dirn
 
-    def ring_step(s, dirns):
-        for piece in range(2):
-            for dirn in dirns:
-                if not used(dirn, s, piece):
-                    continue
-                t = (z + (4 - s if dirn == 0 else 4 + s)) % 8
-                total = mine[piece, t] + fromsib[piece, t]
-                if s > 0 and used(dirn, s - 1, piece):
-                    z_copy(dirn, s - 1, piece).wait_recv()
-                    total = total + zr[dirn, s - 1, piece].astype(F32)
-                zs[dirn, s, piece] = total.astype(BF16)
-                z_copy(dirn, s, piece).start()
+    def plane(piece):
+        return h if piece else 1 - h
+
+    def ring_step(s, dirns, piece):
+        for dirn in dirns:
+            if not used(dirn, s, piece):
+                continue
+            t = (z + (4 - s if dirn == 0 else 4 + s)) % 8
+            total = mine[plane(piece), t] + fromsib[plane(piece), t]
+            if s > 0 and used(dirn, s - 1, piece):
+                z_copy(dirn, s - 1, piece).wait_recv()
+                total = total + zr[dirn, s - 1, piece].astype(F32)
+            zs[dirn, s, piece] = total.astype(BF16)
+            z_copy(dirn, s, piece).start()
 
     for group in range(4):
         lax.fori_loop(2 * group, 2 * group + 2, block_step, 0)
-        for b in (2 * group, 2 * group + 1):
-            sib_copy(b).wait_recv()
-        if group == 0:
-            ring_step(0, (0, 1))
-        elif group == 1:
-            ring_step(1, (0,))
-        elif group == 2:
-            ring_step(1, (1,))
-            ring_step(2, (0, 1))
-        else:
-            ring_step(3, (0, 1))
-    for piece in range(2):
+        s, dirns = ((0, (0, 1)), (1, (0,)), (1, (1,)), (3, (0, 1)))[group]
+        for piece in range(2):
+            sib_copy(2 * group + piece).wait_recv()
+            ring_step(s, dirns, piece)
+        if group == 2:
+            for piece in range(2):
+                ring_step(2, (0, 1), piece)
+
+    def z_total(piece):
         for dirn in range(2):
             z_copy(dirn, 3, piece).wait_recv()
-
-    def z_total(piece):
-        return mine[piece, z] + fromsib[piece, z] + zr[0, 3, piece].astype(F32) + zr[1, 3, piece].astype(F32)
+        at = plane(piece)
+        return mine[at, z] + fromsib[at, z] + zr[0, 3, piece].astype(F32) + zr[1, 3, piece].astype(F32)
 
     pair = rcopy(xs, xrv, hss, hrs, partner)
-    xs[...] = z_total(1 - h)
+    xs[...] = z_total(0)
     pair.start()
-    own_sum = z_total(h)
+    own_sum = z_total(1)
     pair.wait_recv()
     summed = own_sum + xrv[...]
     pseudo = ow[...] - summed / 32
@@ -291,51 +297,50 @@
         for part in range(2):
             ring_arrival(part, d)
 
-    def kx_copy(part, side):
-        return rcopy(ksx.at[part, side], krx.at[part, side], kxs.at[part, side], kxr.at[part, side], high(0) if side else low(0))
-
-    def ky_copy(part, n):
+    def kx_copy(q, side):
+        return rcopy(ksx.at[q, side], krx.at[q, side], kxs.at[q, side], kxr.at[q, side], high(0) if side else low(0))
+
+    def ky_copy(q, n):
         dy = (1, 3, 2)[n]
-        return rcopy(ksy.at[part, (yy + dy) % 4], kry.at[part, yy], kys.at[part, n], kyr.at[part, n], same(dy))
+        return rcopy(ksy.at[q, (yy + dy) % 4], kry.at[q, yy], kys.at[q, n], kyr.at[q, n], same(dy))
+
+    def weight(q):
+        return nw[q // 2, :, :, :, :, pl.ds(q % 2 * QUAD, QUAD)].reshape(BLK, QUAD)
 
     own[1].wait()
     for n in range(11):
         na_copy(n).wait_recv()
-    for part in range(2):
-        for ph in range(2):
-            for pz in range(8):
-                sib_spread(part, ph, pz).wait_recv()
+    for q in range(4):
+        if q % 2 == 0:
+            for ph in range(2):
+                for pz in range(8):
+                    sib_spread(q // 2, ph, pz).wait_recv()
         for side in range(2):
-            rows = pl.ds(512 + side * 256, 256)
-            ksx[part, side] = jnp.dot(nar[rows], nw[part].reshape(BLK, HALF), preferred_element_type=F32).astype(BF16)
-            kx_copy(part, side).start()
+            ksx[q, side] = jnp.dot(nar[pl.ds(512 + side * 256, 256)], weight(q), preferred_element_type=F32).astype(BF16)
+            kx_copy(q, side).start()
     for n in range(9, 11):
         ig_copy(n).start()
-    for part in range(2):
-        def own_step(y, c):
-            acc[part, y] = jnp.dot(nar[at_rows(y * TOK, TOK, TOK)], nw[part].reshape(BLK, HALF), preferred_element_type=F32)
-            return c
-
-        lax.fori_loop(0, 4, own_step, 0)
-    for part in range(2):
+    for q in range(4):
+        acc[q] = jnp.dot(nar[pl.ds(0, 512)], weight(q), preferred_element_type=F32).reshape(4, TOK, QUAD)
+    for q in range(4):
         for side in range(2):
-            kx_copy(part, side).wait_recv()
+            kx_copy(q, side).wait_recv()
 
         def pair_sum(y):
-            other = jnp.concatenate([krx[part, 0, at_rows(y * 64, 64, 64)], krx[part, 1, at_rows(y * 64, 64, 64)]], axis=0)
-            return acc[part, y] + other.astype(F32)
+            other = jnp.concatenate([krx[q, 0, at_rows(y * 64, 64, 64)], krx[q, 1, at_rows(y * 64, 64, 64)]], axis=0)
+            return acc[q, y] + other.astype(F32)
 
         for n in range(3):
             to = (yy + (1, 3, 2)[n]) % 4
-            ksy[part, to] = pair_sum(to).astype(BF16)
-            ky_copy(part, n).start()
-        acc[part, yy] = pair_sum(yy)
-    for part in range(2):
-        total = acc[part, yy]
+            ksy[q, to] = pair_sum(to).astype(BF16)
+            ky_copy(q, n).start()
+        acc[q, yy] = pair_sum(yy)
+    for q in range(4):
+        total = acc[q, yy]
         for n in range(3):
-            ky_copy(part, n).wait_recv()
-            total = total + kry[part, (yy + 4 - (1, 3, 2)[n]) % 4].astype(F32)
-        nk[:, pl.ds(part * HALF, HALF)] = total.astype(BF16)
+            ky_copy(q, n).wait_recv()
+            total = total + kry[q, (yy + 4 - (1, 3, 2)[n]) % 4].astype(F32)
+        nk[:, pl.ds(q * QUAD, QUAD)] = total.astype(BF16)
 
     for n in range(11):
         ig_copy(n).wait_recv()
@@ -372,10 +377,11 @@
         for ph in range(2):
             for pz in range(8):
                 sib_spread(part, ph, pz).wait_send()
+    for q in range(4):
         for side in range(2):
-            kx_copy(part, side).wait_send()
+            kx_copy(q, side).wait_send()
         for n in range(3):
-            ky_copy(part, n).wait_send()
+            ky_copy(q, n).wait_send()
 
 
 def local(activations, cotangent, inner_weight, outer_weight, outer_momentum, next_activations):
@@ -407,19 +413,19 @@
             pltpu.VMEM((SH, KV), F32),
             pltpu.VMEM((SH, KV), F32),
             pltpu.VMEM((2, 2, 8, 2, SH, HALF), BF16),
-            pltpu.VMEM((2, 2, 256, HALF), BF16),
-            pltpu.VMEM((2, 2, 256, HALF), BF16),
-            pltpu.VMEM((2, 4, TOK, HALF), BF16),
-            pltpu.VMEM((2, 4, TOK, HALF), BF16),
-            pltpu.VMEM((2, 4, TOK, HALF), F32),
+            pltpu.VMEM((4, 2, 256, QUAD), BF16),
+            pltpu.VMEM((4, 2, 256, QUAD), BF16),
+            pltpu.VMEM((4, 4, TOK, QUAD), BF16),
+            pltpu.VMEM((4, 4, TOK, QUAD), BF16),
+            pltpu.VMEM((4, 4, TOK, QUAD), F32),
             dma((4,)),
             dma((3,)), dma((3,)),
             dma((3, 4)), dma((3, 4)),
             dma((8, 11)), dma((8, 11)),
             dma((11,)), dma((11,)),
             dma((11,)), dma((11,)),
-            dma((2, 2)), dma((2, 2)),
-            dma((2, 3)), dma((2, 3)),
+            dma((4, 2)), dma((4, 2)),
+            dma((4, 3)), dma((4, 3)),
             dma((8,)), dma((8,)),
             dma((2, 4, 2)), dma((2, 4, 2)),
             dma, dma,

time: 126 us -> 122 us (0.968)
  Pallas kernels: 121 us -> 115 us
    pallas_call x1, Pallas kernels: 121 us -> 115 us  [local(): pl.pallas_call(kernel, out_shape=(jax.ShapeDtypeStruct((TOK, 8 * BLK), BF...]
where the time goes in v3:
time: 122 us; the launch traced here: 121 us
  Pallas kernels  115 us (94%)
  local copies, waits for them, and re-layouts  5.17 us (4%)
    pallas_call x1, Pallas kernels, local(): pl.pallas_call(kernel, out_shape=(jax.ShapeDtypeStruct((TOK, 8 * BLK), BF...  115 us
    unnamed x10, local copies, waits for them, and re-layouts  5.17 us

profile of v3, /device:TPU:8, one launch (start us, length us, event | category | flops | bytes accessed | tf_op | source)
XLA Modules:
  0.0 121.2 jit_solution(10348722190644841991)
XLA Ops:
  0.6 115.3 %shard_map.93 = (bf16[128,8192]{1,0:T(8,128)(2,1)}, bf16[128,1024]{1,0:T(8,128)(2,1)}, f32[32,1024]{1,0:T(8,128)}, f32[32,1024]{1,0:T(8,128)}) custom-call(bf16[128,8192]{1,0:T(8,128)(2,1)} %x.1, bf16[128,1024]{1,0:T(8,128)(2,1)} %g.1, bf16[1,1024,1024]{2,1,0:T(8,128)(2,1)} %w.1, f32[32,1024]{1,0:T(8,128)} %ow.1, f32[32,1024]{1,0:T(8,128)} %om.1, ...), custom_call_target="tpu_custom_call" | custom-call | tf_op jit(solution)/shard_map/pallas_call | solution.py:391
  116.0 0.0 copy-start
  116.0 0.0 copy-start.2
  116.0 0.0 copy-start.1
  116.0 3.1 %copy.14 = bf16[128,8192]{1,0:T(8,128)(2,1)} copy(bf16[128,8192]{1,0:T(8,128)(2,1)} %get-tuple-element.8) | data formatting | bytes 4194304
  119.2 0.0 copy-done
  119.2 0.7 copy.15
  119.9 0.0 copy-done.2
  119.9 0.7 copy.16
  120.5 0.0 copy-done.1
  120.5 0.7 copy.17
Async XLA Ops:
  116.0 3.2 %copy-start = (bf16[128,1024]{1,0:T(8,128)(2,1)S(1)}, bf16[128,1024]{1,0:T(8,128)(2,1)}, u32[]{:S(2)}) copy-start(bf16[128,1024]{1,0:T(8,128)(2,1)} %get-tuple-element.9) | copy-start | bytes 786436
  116.0 3.9 %copy-start.2 = (f32[32,1024]{1,0:T(8,128)S(1)}, f32[32,1024]{1,0:T(8,128)}, u32[]{:S(2)}) copy-start(f32[32,1024]{1,0:T(8,128)} %get-tuple-element.10) | copy-start | bytes 393220
  116.0 4.5 %copy-start.1 = (f32[32,1024]{1,0:T(8,128)S(1)}, f32[32,1024]{1,0:T(8,128)}, u32[]{:S(2)}) copy-start(f32[32,1024]{1,0:T(8,128)} %get-tuple-element.11) | copy-start | bytes 393220

commit v4 on v3

--- a/solution.py
+++ b/solution.py
@@ -157,6 +157,8 @@
         na_copy(n).start()
     for n in range(3, 7):
         ig_copy(n).start()
+    for n in range(3):
+        ig_copy(n).start()
 
     own[0].wait()
 
@@ -268,8 +270,6 @@
         cross(part).wait_recv()
         ring_first(part, 1 - h)
         sib_spread(part, 1 - h, z).start()
-    for n in range(3):
-        ig_copy(n).start()
     for y in range(4):
         gx_copy(2, y).wait_recv()
 
@@ -278,7 +278,7 @@
         return c
 
     lax.fori_loop(0, 2, late_step, 0)
-    for n in range(7, 9):
+    for n in range(7, 11):
         ig_copy(n).start()
     ig_own = pltpu.make_async_copy(igs.at[at_rows(yy * TOK, TOK, TOK)], ig.at[:, cols(f)], loc.at[3])
     ig_own.start()
@@ -318,8 +318,6 @@
         for side in range(2):
             ksx[q, side] = jnp.dot(nar[pl.ds(512 + side * 256, 256)], weight(q), preferred_element_type=F32).astype(BF16)
             kx_copy(q, side).start()
-    for n in range(9, 11):
-        ig_copy(n).start()
     for q in range(4):
         acc[q] = jnp.dot(nar[pl.ds(0, 512)], weight(q), preferred_element_type=F32).reshape(4, TOK, QUAD)
     for q in range(4):
@@ -382,6 +380,37 @@
             kx_copy(q, side).wait_send()
         for n in range(3):
             ky_copy(q, n).wait_send()
+
+
+def move(*refs):
+    sources, targets, (wide, keys, outer, momentum, got, put) = refs[:4], refs[4:8], refs[8:]
+    steps = []
+    for n in range(8):
+        at = (slice(None), pl.ds(n * BLK, BLK))
+        steps.append((sources[0].at[at], wide.at[at], targets[0].at[at]))
+    for source, between, target in zip(sources[1:], (keys, outer, momentum), targets[1:]):
+        steps.append((source, between, target))
+    into = [pltpu.make_async_copy(a, b, got.at[n]) for n, (a, b, _) in enumerate(steps)]
+    out = [pltpu.make_async_copy(b, c, put.at[n]) for n, (_, b, c) in enumerate(steps)]
+    for copy in into:
+        copy.start()
+    for n, copy in enumerate(into):
+        copy.wait()
+        out[n].start()
+    for copy in out:
+        copy.wait()
+
+
+def hand_over(arrays):
+    hb = pl.BlockSpec(memory_space=pl.ANY)
+    return pl.pallas_call(
+        move,
+        out_shape=tuple(jax.ShapeDtypeStruct(a.shape, a.dtype) for a in arrays),
+        in_specs=[hb] * 4,
+        out_specs=(hb,) * 4,
+        scratch_shapes=[pltpu.VMEM(a.shape, a.dtype) for a in arrays]
+        + [pltpu.SemaphoreType.DMA((11,)), pltpu.SemaphoreType.DMA((11,))],
+    )(*arrays)
 
 
 def local(activations, cotangent, inner_weight, outer_weight, outer_momentum, next_activations):
@@ -435,7 +464,7 @@
         ],
         compiler_params=pltpu.CompilerParams(collective_id=0, has_side_effects=True, vmem_limit_bytes=60 * 1024 * 1024),
     )(activations, cotangent, inner_weight, outer_weight, outer_momentum, next_activations)
-    return ig, nk, no, nm
+    return hand_over((ig, nk, no, nm))
 
 
 def solution(mesh):

time: 122 us -> 118 us (0.967)
  local copies, waits for them, and re-layouts: 5.17 us -> 0 us
  Pallas kernels: 115 us -> 117 us
    unnamed x10 -> x0, local copies, waits for them, and re-layouts: 5.17 us -> none
    pallas_call x0 -> x1, Pallas kernels: none -> 2.62 us  [hand_over(): pl.pallas_call(move, out_shape=tuple((jax.ShapeDtypeStruct(a.shape, a.dty...]
where the time goes in v4:
time: 118 us
  Pallas kernels  117 us (99%)
    pallas_call x1, Pallas kernels, local(): pl.pallas_call(kernel, out_shape=(jax.ShapeDtypeStruct((TOK, 8 * BLK), BF...  114 us
    pallas_call x1, Pallas kernels, hand_over(): pl.pallas_call(move, out_shape=tuple((jax.ShapeDtypeStruct(a.shape, a.dty...  2.62 us

profile of v4, /device:TPU:8, one launch (start us, length us, event | category | flops | bytes accessed | tf_op | source)
XLA Modules:
  0.0 117.6 jit_solution(17748428771602238228)
XLA Ops:
  0.6 114.4 %shard_map.93 = (bf16[128,8192]{1,0:T(8,128)(2,1)}, bf16[128,1024]{1,0:T(8,128)(2,1)}, f32[32,1024]{1,0:T(8,128)}, f32[32,1024]{1,0:T(8,128)}) custom-call(bf16[128,8192]{1,0:T(8,128)(2,1)} %x.1, bf16[128,1024]{1,0:T(8,128)(2,1)} %g.1, bf16[1,1024,1024]{2,1,0:T(8,128)(2,1)} %w.1, f32[32,1024]{1,0:T(8,128)} %ow.1, f32[32,1024]{1,0:T(8,128)} %om.1, ...), custom_call_target="tpu_custom_call" | custom-call | tf_op jit(solution)/shard_map/pallas_call | solution.py:420
  115.0 2.6 %shard_map.94 = (bf16[128,8192]{1,0:T(8,128)(2,1)}, bf16[128,1024]{1,0:T(8,128)(2,1)}, f32[32,1024]{1,0:T(8,128)}, f32[32,1024]{1,0:T(8,128)}) custom-call(bf16[128,8192]{1,0:T(8,128)(2,1)} %get-tuple-element.8.refs_0_, bf16[128,1024]{1,0:T(8,128)(2,1)} %get-tuple-element.9.refs_1_, f32[32,1024]{1,0:T(8,128)} %get-tuple-element.10.refs_2_, ...), custom_call_target="tpu_custom_call" | custom-call | tf_op jit(solution)/shard_map/pallas_call | solution.py:406

commit v5 on v4

--- a/solution.py
+++ b/solution.py
@@ -17,7 +17,8 @@
 SH = 32
 HALF = 512
 QUAD = 256
-XEARLY = 4
+XEARLY = 2
+XMID = 2
 F32 = jnp.float32
 BF16 = jnp.bfloat16
 MESH = pl.DeviceIdType.MESH
@@ -52,8 +53,8 @@
         {"island": h * 16 + ((z + 7) % 8) * 2 + core, "fsdp": f},
     ]
     routes = [(same(dy), 0, TOK, yy * TOK) for dy in (1, 3, 2)]
-    routes += [(low(dy), 0, 64, 512 + yy * 64) for dy in range(4)]
-    routes += [(high(dy), 64, 64, 768 + yy * 64) for dy in range(4)]
+    for dy in range(4):
+        routes += [(low(dy), 0, 64, 512 + yy * 64), (high(dy), 64, 64, 768 + yy * 64)]
 
     def at_rows(start, size, step):
         return pl.ds(pl.multiple_of(start, step), size)
@@ -67,7 +68,9 @@
     w_load = pltpu.make_async_copy(w.at[0], wv, loc.at[0])
     own = [pltpu.make_async_copy(x.at[:, cols(f)], xr.at[at_rows(yy * TOK, TOK, TOK)], loc.at[1]),
            pltpu.make_async_copy(na.at[:, cols(f)], nar.at[at_rows(yy * TOK, TOK, TOK)], loc.at[2])]
+    g_own = pltpu.make_async_copy(g, gr.at[at_rows(yy * TOK, TOK, TOK)], loc.at[2 + 2])
     w_load.start()
+    g_own.start()
     own[0].start()
     own[1].start()
 
@@ -78,6 +81,10 @@
 
     def gy_copy(n):
         return rcopy(g, gr.at[at_rows(yy * TOK, TOK, TOK)], gys.at[n], gyr.at[n], routes[n][0])
+
+    def gz_copy(n):
+        rows = at_rows(((yy + (3, 1)[n]) % 4) * TOK + n * 64, 64, 64)
+        return rcopy(gr.at[rows], gr.at[rows], gys.at[2 + n], gyr.at[2 + n], routes[n][0])
 
     def gx_copy(n, y):
         src = gr.at[at_rows(y * TOK + (0 if n == 0 else 64), 64, 64)]
@@ -93,7 +100,7 @@
 
     def x_copy(b, n):
         bh, bz = block_place(b)
-        if n >= 7:
+        if n >= 3 and n % 2 == 0:
             bh = 1 - bh
         row = bh * 512 + bz * 128
         dev, first, size, to = routes[n]
@@ -121,19 +128,24 @@
 
         return body
 
-    for n in range(3):
+    for n in range(2):
         gy_copy(n).start()
-    gr[at_rows(yy * TOK, TOK, TOK)] = g[...]
+    g_own.wait()
     for n in range(2):
         rcopy(g.at[pl.ds(n * 64, 64)], gr.at[at_rows(512 + n * 256 + yy * 64, 64, 64)], gxs.at[n, yy], gxr.at[n, yy],
               high(0) if n == 1 else low(0)).start()
     lax.fori_loop(0, XEARLY, send_x(range(3)), 0)
-    for n, dy in enumerate((1, 3, 2)):
+    for n, dy in enumerate((1, 3)):
         gy_copy(n).wait_recv()
+        gz_copy(n).start()
         for m in range(2):
             gx_copy(m, (yy + 4 - dy) % 4).start()
     lax.fori_loop(0, XEARLY, send_x(range(3, 11)), 0)
-    lax.fori_loop(XEARLY, 8, send_x(range(11)), 0)
+    lax.fori_loop(XEARLY, XMID, send_x(range(11)), 0)
+    for n in range(2):
+        gz_copy(n).wait_recv()
+        gx_copy(n, (yy + 2) % 4).start()
+    lax.fori_loop(XMID, 8, send_x(range(11)), 0)
     rcopy(g.at[pl.ds(64, 64)], glo.at[at_rows(yy * 64, 64, 64)], gxs.at[2, yy], gxr.at[2, yy], low(0)).start()
     for dy in (1, 3, 2):
         gx_copy(2, (yy + 4 - dy) % 4).start()
@@ -346,8 +358,10 @@
     for n in range(11):
         ig_copy(n).wait_send()
         na_copy(n).wait_send()
+    for n in range(2):
+        gy_copy(n).wait_send()
+        gz_copy(n).wait_send()
     for n in range(3):
-        gy_copy(n).wait_send()
         for y in range(4):
             gx_copy(n, y).wait_send()
 
@@ -425,7 +439,7 @@
             jax.ShapeDtypeStruct((SH, KV), F32),
             jax.ShapeDtypeStruct((SH, KV), F32),
         ),
-        in_specs=[hb, vm, hb, vm, vm, hb],
+        in_specs=[hb, hb, hb, vm, vm, hb],
         out_specs=(hb, vm, vm, vm),
         scratch_shapes=[
             pltpu.VMEM((BLK, KV), BF16),
@@ -447,8 +461,8 @@
             pltpu.VMEM((4, 4, TOK, QUAD), BF16),
             pltpu.VMEM((4, 4, TOK, QUAD), BF16),
             pltpu.VMEM((4, 4, TOK, QUAD), F32),
-            dma((4,)),
-            dma((3,)), dma((3,)),
+            dma((5,)),
+            dma((4,)), dma((4,)),
             dma((3, 4)), dma((3, 4)),
             dma((8, 11)), dma((8, 11)),
             dma((11,)), dma((11,)),

time: 118 us -> 116 us (0.983)
  Pallas kernels: 117 us -> 115 us
    pallas_call x1, Pallas kernels: 114 us -> 112 us  [local(): pl.pallas_call(kernel, out_shape=(jax.ShapeDtypeStruct((TOK, 8 * BLK), BF...]
where the time goes in v5:
time: 116 us; the launch traced here: 115 us
  Pallas kernels  115 us (99%)
    pallas_call x1, Pallas kernels, local(): pl.pallas_call(kernel, out_shape=(jax.ShapeDtypeStruct((TOK, 8 * BLK), BF...  112 us
    pallas_call x1, Pallas kernels, hand_over(): pl.pallas_call(move, out_shape=tuple((jax.ShapeDtypeStruct(a.shape, a.dty...  2.62 us

profile of v5, /device:TPU:8, one launch (start us, length us, event | category | flops | bytes accessed | tf_op | source)
XLA Modules:
  0.0 115.4 jit_solution(2470834345768770109)
XLA Ops:
  0.6 112.2 %shard_map.93 = (bf16[128,8192]{1,0:T(8,128)(2,1)}, bf16[128,1024]{1,0:T(8,128)(2,1)}, f32[32,1024]{1,0:T(8,128)}, f32[32,1024]{1,0:T(8,128)}) custom-call(bf16[128,8192]{1,0:T(8,128)(2,1)} %x.1, bf16[128,1024]{1,0:T(8,128)(2,1)} %g.1, bf16[1,1024,1024]{2,1,0:T(8,128)(2,1)} %w.1, f32[32,1024]{1,0:T(8,128)} %ow.1, f32[32,1024]{1,0:T(8,128)} %om.1, ...), custom_call_target="tpu_custom_call" | custom-call | tf_op jit(solution)/shard_map/pallas_call | solution.py:434
  112.8 2.6 %shard_map.94 = (bf16[128,8192]{1,0:T(8,128)(2,1)}, bf16[128,1024]{1,0:T(8,128)(2,1)}, f32[32,1024]{1,0:T(8,128)}, f32[32,1024]{1,0:T(8,128)}) custom-call(bf16[128,8192]{1,0:T(8,128)(2,1)} %get-tuple-element.8.refs_0_, bf16[128,1024]{1,0:T(8,128)(2,1)} %get-tuple-element.9.refs_1_, f32[32,1024]{1,0:T(8,128)} %get-tuple-element.10.refs_2_, ...), custom_call_target="tpu_custom_call" | custom-call | tf_op jit(solution)/shard_map/pallas_call | solution.py:420

commit v6 on v5

--- a/solution.py
+++ b/solution.py
@@ -17,8 +17,8 @@
 SH = 32
 HALF = 512
 QUAD = 256
-XEARLY = 2
-XMID = 2
+XEARLY = 3
+XMID = 3
 F32 = jnp.float32
 BF16 = jnp.bfloat16
 MESH = pl.DeviceIdType.MESH

time: 116 us -> 114 us (0.983); the launches traced: 115 us -> 112 us
  Pallas kernels: 115 us -> 112 us
    pallas_call x1, Pallas kernels: 112 us -> 109 us  [local(): pl.pallas_call(kernel, out_shape=(jax.ShapeDtypeStruct((TOK, 8 * BLK), BF...]
where the time goes in v6:
time: 114 us; the launch traced here: 112 us
  Pallas kernels  112 us (98%)
    pallas_call x1, Pallas kernels, local(): pl.pallas_call(kernel, out_shape=(jax.ShapeDtypeStruct((TOK, 8 * BLK), BF...  109 us
    pallas_call x1, Pallas kernels, hand_over(): pl.pallas_call(move, out_shape=tuple((jax.ShapeDtypeStruct(a.shape, a.dty...  2.62 us

profile of v6, /device:TPU:8, one launch (start us, length us, event | category | flops | bytes accessed | tf_op | source)
XLA Modules:
  0.0 112.3 jit_solution(17747136347021949155)
XLA Ops:
  0.6 109.0 %shard_map.93 = (bf16[128,8192]{1,0:T(8,128)(2,1)}, bf16[128,1024]{1,0:T(8,128)(2,1)}, f32[32,1024]{1,0:T(8,128)}, f32[32,1024]{1,0:T(8,128)}) custom-call(bf16[128,8192]{1,0:T(8,128)(2,1)} %x.1, bf16[128,1024]{1,0:T(8,128)(2,1)} %g.1, bf16[1,1024,1024]{2,1,0:T(8,128)(2,1)} %w.1, f32[32,1024]{1,0:T(8,128)} %ow.1, f32[32,1024]{1,0:T(8,128)} %om.1, ...), custom_call_target="tpu_custom_call" | custom-call | tf_op jit(solution)/shard_map/pallas_call | solution.py:434
  109.7 2.6 %shard_map.94 = (bf16[128,8192]{1,0:T(8,128)(2,1)}, bf16[128,1024]{1,0:T(8,128)(2,1)}, f32[32,1024]{1,0:T(8,128)}, f32[32,1024]{1,0:T(8,128)}) custom-call(bf16[128,8192]{1,0:T(8,128)(2,1)} %get-tuple-element.8.refs_0_, bf16[128,1024]{1,0:T(8,128)(2,1)} %get-tuple-element.9.refs_1_, f32[32,1024]{1,0:T(8,128)} %get-tuple-element.10.refs_2_, ...), custom_call_target="tpu_custom_call" | custom-call | tf_op jit(solution)/shard_map/pallas_call | solution.py:420
